TPU v7x, 128 devices: a whole 4x4x4 slice. The times are simulated.
128 devices in a mesh: blk: 32 (over x, y, core), mp: 4 (over z).
Axes of the slice: x: 4, y: 4, z: 4, core: 2. Of those that a mesh axis runs over, the one named last changes fastest.
Arguments:
- hidden: bfloat16 [144, 3584], replicated, may hold values from -6 to 6
- medusa_w: bfloat16 [2, 3584, 3584], P(None, 'blk', 'mp'), may hold values from -0.09375 to 0.09375
- embedding: bfloat16 [131072, 3584], P(('blk', 'mp')), may hold values from -0.5 to 0.5
- cand_ids: int32 [2, 144, 10], replicated, may hold values from 0 to 131071
- tree_q: bfloat16 [12, 48, 4096], P(None, None, 'mp'), may hold values from -6 to 6
- tree_key_value: bfloat16 [2, 12, 48, 2048], P(None, None, None, 'mp'), may hold values from -6 to 6
- prompt_key_value: bfloat16 [2, 32, 2048, 2048], P(None, 'blk', None, 'mp'), may hold values from -6 to 6
- block_group: int32 [32], P('blk'), may hold values from 0 to 11, as said below
- block_len: int32 [32], P('blk'), may hold values from 1 to 2048
- block_empty: int32 [32], P('blk'), may hold values 0 or 1
- parents: int32 [12, 48], replicated, may hold values from 0 to 46, as said below
- out_weight: bfloat16 [4096, 3584], P('mp'), may hold values from -0.09375 to 0.09375
- post_gain: float32 [3584], replicated, may hold values from 0.5 to 1.5
- resid: bfloat16 [576, 3584], P('blk'), may hold values from -6 to 6
Outputs:
- draft_logprob: float32 [2, 144, 10], replicated
- layer_out: bfloat16 [576, 3584], P('blk')
Inputs may be any that keep to these rules, and one draw needn't show every extreme that they name: `block_group`: every group number from 0 to min(12, 32) - 1 owns at least one block. `parents`: entry 0 of each row is 0; entry i for i >= 1 is below i; some group's last token has parent 48 - 2.
All inputs are finite; a program needn't handle non-finite values. No bound on the sum of `block_empty` on one device may be relied on, other than what follows from the above.
Results may differ from a plain program's by a relative error of at most 0.005.
Values may be sent and summed in bfloat16 or wider, within the bound.
A program may use at most 128 MiB of HBM per device.

v0:
```python
import jax
import jax.numpy as jnp
from jax import lax
from jax.sharding import PartitionSpec as P

HEAD_SIZE = 256


def capped(values, limit):
    return limit * jnp.tanh(values / limit)


def ancestry(parents):
    count = parents.shape[1]
    column = jnp.arange(count, dtype=jnp.int32)
    linked = (parents[:, :, None] == column[None, None, :]) & (column[None, :, None] > 0)
    reach = jnp.eye(count, dtype=jnp.float32)[None] + linked.astype(jnp.float32)
    for sweep in range(count.bit_length()):
        reach = jnp.minimum(
            jnp.einsum("gij,gjk->gik", reach, reach, precision=lax.Precision.HIGHEST), 1.0
        )
    return reach


def attend(queries, keys, values, mask):
    rows = queries.shape[0]
    length = keys.shape[0]
    kv_heads = keys.shape[1] // HEAD_SIZE
    repeats = queries.shape[1] // keys.shape[1]
    query_view = queries.reshape(rows, kv_heads, repeats, HEAD_SIZE)
    key_view = keys.reshape(length, kv_heads, HEAD_SIZE)
    value_view = values.reshape(length, kv_heads, HEAD_SIZE)
    scores = jnp.einsum(
        "qhrd,khd->hrqk", query_view, key_view, preferred_element_type=jnp.float32
    ) * HEAD_SIZE ** (-0.5)
    weights = jnp.exp(capped(scores, 50.0)) * mask[None, None]
    denominator = jnp.sum(weights, -1).transpose(2, 0, 1).reshape(rows, kv_heads * repeats)
    numerator = jnp.einsum(
        "hrqk,khd->qhrd",
        weights.astype(jnp.bfloat16),
        value_view,
        preferred_element_type=jnp.float32,
    )
    return (numerator.reshape(rows, kv_heads * repeats * HEAD_SIZE), denominator)


def per_device(
    hidden,
    medusa_w,
    embedding,
    cand_ids,
    tree_q,
    tree_key_value,
    prompt_key_value,
    block_group,
    block_len,
    block_empty,
    parents,
    out_weight,
    post_gain,
    resid,
):
    units = medusa_w.shape[2]
    inner = jnp.einsum(
        "rd,mdu->mru",
        hidden,
        lax.all_gather(medusa_w, "blk", axis=1, tiled=True),
        preferred_element_type=jnp.float32,
    )
    own_cols = lax.dynamic_slice_in_dim(hidden, lax.axis_index("mp") * units, units, 1).astype(
        jnp.float32
    )
    fresh = (own_cols[None] + jax.nn.silu(inner)).astype(jnp.bfloat16)
    full_fresh = lax.all_gather(fresh, "mp", axis=2, tiled=True)
    logits = capped(
        jnp.einsum("mrd,vd->mrv", full_fresh, embedding, preferred_element_type=jnp.float32), 30.0
    )
    totals = jnp.sum(jnp.exp(logits), -1)
    vocab_dev = embedding.shape[0]
    first_id = lax.axis_index(("blk", "mp")) * vocab_dev
    local_ids = cand_ids - first_id
    match = local_ids[..., None] == jnp.arange(vocab_dev, dtype=jnp.int32)
    picked = jnp.sum(jnp.where(match, logits[:, :, None, :], 0.0), -1)
    totals, picked = lax.psum((totals, picked), ("blk", "mp"))
    draft_logprob = picked - jnp.log(totals)[..., None]
    groups, tree_size, features = tree_q.shape
    keys = prompt_key_value[0, 0]
    values = prompt_key_value[1, 0]
    length = keys.shape[0]
    group = block_group[0]
    key_ok = ((jnp.arange(length, dtype=jnp.int32) < block_len[0]) & (block_empty[0] == 0)).astype(
        jnp.float32
    )
    row_group = jnp.arange(groups * tree_size, dtype=jnp.int32) // tree_size
    mask = (row_group == group).astype(jnp.float32)[:, None] * key_ok[None, :]
    numer, denom = attend(tree_q.reshape(groups * tree_size, features), keys, values, mask)
    rows_dev = groups * tree_size // lax.axis_size("blk")
    first_row = lax.axis_index("blk") * rows_dev
    summed = lax.psum((numer, denom), "blk")
    numer = lax.dynamic_slice_in_dim(summed[0], first_row, rows_dev, 0)
    denom = lax.dynamic_slice_in_dim(summed[1], first_row, rows_dev, 0)
    reach = ancestry(parents)
    tree_numer, tree_denom = jax.vmap(attend)(tree_q, tree_key_value[0], tree_key_value[1], reach)
    heads_dev = tree_denom.shape[2]
    tree_numer = lax.dynamic_slice_in_dim(
        tree_numer.reshape(groups * tree_size, features), first_row, rows_dev, 0
    )
    tree_denom = lax.dynamic_slice_in_dim(
        tree_denom.reshape(groups * tree_size, heads_dev), first_row, rows_dev, 0
    )
    numer = numer + tree_numer
    denom = denom + tree_denom
    heads_out = (
        (numer.reshape(rows_dev, heads_dev, HEAD_SIZE) / denom[..., None])
        .reshape(rows_dev, features)
        .astype(jnp.bfloat16)
    )
    attn = lax.psum(jnp.dot(heads_out, out_weight, preferred_element_type=jnp.float32), "mp")
    normed = attn * lax.rsqrt(jnp.mean(attn * attn, -1, keepdims=True) + 1e-06) * post_gain
    layer_out = (normed + resid.astype(jnp.float32)).astype(jnp.bfloat16)
    return (draft_logprob, layer_out)


def solution(mesh):
    placed = (
        P(),
        P(None, "blk", "mp"),
        P(("blk", "mp"), None),
        P(),
        P(None, None, "mp"),
        P(None, None, None, "mp"),
        P(None, "blk", None, "mp"),
        P("blk"),
        P("blk"),
        P("blk"),
        P(),
        P("mp", None),
        P(),
        P("blk", None),
    )
    return jax.shard_map(
        per_device, mesh=mesh, in_specs=placed, out_specs=(P(), P("blk", None)), check_vma=False
    )
```

profile of v0, /device:TPU:1, one launch (start us, length us, event | category | flops | bytes accessed | tf_op | source)
XLA Modules:
  0.0 381.7 jit_solution(4261685247920140671)
XLA Ops:
  7.2 0.0 all-reduce.4.cloned.1.call-start
  7.2 4.4 %fusion.51 = (bf16[1,1,2048,512]{3,2,1,0:T(8,128)(2,1)}, bf16[1,1,2048,512]{3,2,1,0:T(8,128)(2,1)}) fusion(bf16[2,1,2048,512]{3,2,1,0:T(8,128)(2,1)} %param.20), kind=kLoop, calls=%fused_computation.70 | loop fusion | bytes 8388608 | tf_op jit(solution)/shard_map/slice | solution.py:88
  11.6 2.9 copy.79
  16.5 3.3 reshape_reshape.3
  19.8 4.0 %copy.80 = bf16[1,1,2048,512]{2,3,1,0:T(8,128)(2,1)} copy(bf16[1,1,2048,512]{3,2,1,0:T(8,128)(2,1)} %get-tuple-element.6) | data formatting | bytes 4194304
  23.8 0.4 broadcast_multiply_fusion
  24.2 10.5 %fusion = (f32[2,2,576]{2,1,0:T(2,128)}, f32[2,2048,576,2]{1,2,3,0:T(8,128)}) fusion(f32[576,2048]{1,0:T(8,128)S(1)} %broadcast_multiply_fusion, bf16[2048,2,256,1]{0,2,3,1:T(8,128)(2,1)S(1)} %bitcast.83, bf16[576,2,2,256]{3,2,1,0:T(2,128)(2,1)S(1)} %reshape_reshape.3), kind=kOutput, calls=%fused_computation.1 | convolution fusion | flops 2434791168 | bytes 26878976 | tf_op jit(solution)/shard_map/qhrd,khd->hrqk/dot_general | solution.py:33
  34.7 9.1 %fusion.6 = f32[576,2,2,256]{3,0,2,1:T(8,128)S(1)} fusion(bf16[2048,2,256,1]{0,2,3,1:T(8,128)(2,1)S(1)} %bitcast.85, f32[2,2048,576,2]{1,2,3,0:T(8,128)} %get-tuple-element.15, f32[576,2048]{1,0:T(8,128)S(1)} %broadcast_multiply_fusion), kind=kOutput, calls=%fused_computation.10 | convolution fusion | flops 2434793472 | bytes 28049408 | tf_op jit(solution)/shard_map/hrqk,khd->qhrd/dot_general | solution.py:38
  43.8 1.8 copy.56
  45.6 2.9 reshape.101
  48.6 0.0 all-gather.3.cloned.1.call-start
  48.6 0.7 all-gather.3.cloned.1.call-update
  49.3 0.2 all-reduce.6.cloned.1.call-start
  49.6 0.3 copy-done
  49.8 0.9 reshape.102
  50.7 0.7 reshape.104
  51.4 0.1 fusion.52
  51.5 0.1 reshape_squeeze.14
  51.7 1.4 convolution_minimum_fusion.5
  53.1 0.4 convolution_minimum_fusion.4
  53.5 0.4 convolution_minimum_fusion.3
  53.9 0.4 convolution_minimum_fusion.2
  54.4 0.4 convolution_minimum_fusion.1
  54.8 0.4 convolution_minimum_fusion
  55.2 0.1 copy.59
  55.3 0.9 fusion.53
  56.2 0.1 reshape.105
  56.3 124.9 %psum.38 = f32[576,4]{0,1:T(4,128)S(1)} all-reduce(f32[576,4]{0,1:T(4,128)S(1)} %reshape.104), channel_id=1, replica_groups=mesh['blk'=32,'mp'=4] {'blk'}, use_global_device_ids=true, to_apply=%region_6.7 | all-reduce | flops 2304 | bytes 18432 | tf_op jit(solution)/shard_map/psum | solution.py:99
  181.2 0.1 dynamic-slice_add_fusion
  181.3 0.1 copy.64
  181.4 0.1 div.48
  181.5 0.1 reshape_squeeze.15
  181.7 0.5 convolution_bitcast_fusion
  182.2 1.8 copy.62
  184.1 2.9 reshape.103
  187.0 0.0 all-reduce.4.cloned.1.call-done
  187.1 5.1 %fusion.39 = f32[18,3584]{1,0:T(8,128)} fusion(bf16[1024,3584]{1,0:T(8,128)(2,1)} %param.25, f32[18,1024]{1,0:T(8,128)S(1)} %bitcast.87, f32[576,1024]{1,0:T(8,128)} %reshape.103, s32[]{:T(128)S(6)} %select_n.25, f32[576,1024]{1,0:T(8,128)} %all-reduce.4.cloned.1.call-done), kind=kOutput, calls=%fused_computation.47 | convolution fusion | flops 132175872 | bytes 7868420 | tf_op jit(solution)/shard_map/dot_general | solution.py:118
  192.2 0.3 all-gather.5.cloned.1.call-start
  192.4 32.7 %all-gather.3.cloned.1.call-done = bf16[2,3584,896]{2,1,0:T(8,128)(2,1)} async-done(((bf16[2,112,896]{2,1,0:T(8,128)(2,1)}), bf16[2,3584,896]{2,1,0:T(8,128)(2,1)}) %all-gather.3.cloned.1.call-update) | async-done | bytes 12845072 | tf_op jit(solution)/shard_map/all_gather | solution.py:67
  225.2 7.6 %add_convert_fusion = bf16[2,144,896]{2,1,0:T(8,128)(2,1)} fusion(bf16[2,3584,896]{2,1,0:T(8,128)(2,1)} %all-gather.3.cloned.1.call-done, bf16[144,3584]{1,0:T(8,128)(2,1)S(1)} %copy-done.4, f32[144,896]{1,0:T(8,128)S(1)} %dynamic-slice_convert_fusion), kind=kOutput, calls=%fused_computation.32 | convolution fusion | flops 1851236352 | bytes 14909440 | tf_op jit(solution)/shard_map/rd,mdu->mru/dot_general | solution.py:64
  232.8 34.1 %all-reduce.6.cloned.1.call-done = f32[18,3584]{1,0:T(8,128)} async-done(((f32[18,3584]{1,0:T(8,128)}), f32[18,3584]{1,0:T(8,128)}) %all-reduce.6.cloned.1.call-update) | async-done | bytes 258064 | tf_op jit(solution)/shard_map/psum | solution.py:118
  266.9 1.1 multiply_reduce_fusion
  268.0 1.8 add_convert_fusion.1
  269.8 31.7 %all-gather.5.cloned.1.call-done = bf16[2,144,3584]{2,1,0:T(8,128)(2,1)} async-done(((bf16[2,144,896]{2,1,0:T(8,128)(2,1)}), bf16[2,144,3584]{2,1,0:T(8,128)(2,1)}) %all-gather.5.cloned.1.call-update) | async-done | bytes 2064400 | tf_op jit(solution)/shard_map/all_gather | solution.py:74
  301.5 6.2 %exponential_reduce_fusion = (f32[2,144]{1,0:T(2,128)S(1)}, f32[2,144,1024]{2,1,0:T(8,128)S(1)}) fusion(bf16[2,144,3584]{2,1,0:T(8,128)(2,1)} %all-gather.5.cloned.1.call-done, bf16[1024,3584]{1,0:T(8,128)(2,1)} %param.16), kind=kOutput, calls=%fused_computation.24 | convolution fusion | flops 2114813696 | bytes 10585216 | tf_op jit(solution)/shard_map/mrd,vd->mrv/dot_general | solution.py:76
  307.8 1.8 select_reduce_fusion
  309.6 64.9 %all-reduce = (f32[2,144,10]{1,2,0:T(8,128)S(1)}, f32[2,144]{1,0:T(2,128)S(1)}) all-reduce(f32[2,144,10]{1,2,0:T(8,128)S(1)} %select_reduce_fusion, f32[2,144]{1,0:T(2,128)S(1)} %get-tuple-element.10), channel_id=1, replica_groups=mesh['blk'=32,'mp'=4] {'blk','mp'}, use_global_device_ids=true, to_apply=%region_1.2 | all-reduce | flops 3168 | bytes 25344 | tf_op jit(solution)/shard_map/psum | solution.py:84
  374.5 0.6 copy.65
  (29 shorter events, 0.2 us)
Async XLA Ops:
  7.2 179.9 %all-reduce.4.cloned.1.call-start = ((), (), s32[]{:S(2)}) async-start(), calls=%async_computation.2 | async-start | bytes 4718592 | tf_op jit(solution)/shard_map/psum | solution.py:99
  24.2 10.5 %copy-start.1 = (bf16[1,1,2048,512]{2,3,1,0:T(8,128)(2,1)S(1)}, bf16[1,1,2048,512]{2,3,1,0:T(8,128)(2,1)}, u32[]{:S(2)}) copy-start(bf16[1,1,2048,512]{2,3,1,0:T(8,128)(2,1)} %copy.80) | copy-start | bytes 6291460
  48.6 1.3 copy-start
  48.6 2.9 copy-start.2
  48.6 176.6 %all-gather.3.cloned.1.call-start = ((), (), s32[]{:S(2)}) async-start(), calls=%async_computation | async-start | bytes 13246464 | tf_op jit(solution)/shard_map/all_gather | solution.py:67
  49.3 217.6 %all-reduce.6.cloned.1.call-start = ((), (), s32[]{:S(2)}) async-start(), calls=%async_computation.3 | async-start | bytes 688128 | tf_op jit(solution)/shard_map/psum | solution.py:118
  184.0 3.0 copy-start.4
  192.1 40.7 %copy-start.5 = (s32[2,144,10]{1,0,2:T(2,128)S(1)}, s32[2,144,10]{1,0,2:T(2,128)}, u32[]{:S(2)}) copy-start(s32[2,144,10]{1,0,2:T(2,128)} %param.17) | copy-start | bytes 34564
  192.2 75.9 %copy-start.3 = (bf16[18,3584]{1,0:T(8,128)(2,1)S(1)}, bf16[18,3584]{1,0:T(8,128)(2,1)}, u32[]{:S(2)}) copy-start(bf16[18,3584]{1,0:T(8,128)(2,1)} %param.27) | copy-start | bytes 387076
  192.2 75.9 %copy-start.6 = (f32[3584]{0:T(1024)S(1)}, f32[3584]{0:T(1024)}, u32[]{:S(2)}) copy-start(f32[3584]{0:T(1024)} %param.26) | copy-start | bytes 43012
  192.2 109.4 %all-gather.5.cloned.1.call-start = ((), (), s32[]{:S(2)}) async-start(), calls=%async_computation.1 | async-start | bytes 2580480 | tf_op jit(solution)/shard_map/all_gather | solution.py:74
Sparse Core Ops, SparseCore 0:
  48.7 110.4 all-reduce.3
  161.6 63.5 all-gather.2
  227.5 39.3 all-reduce.5
  268.4 33.0 all-gather.4
where the time goes:
time: 382 us
  blocking collectives  190 us (50%)
  waiting for transfers between devices  99.3 us (26%)
  matrix products  43.3 us (11%)
  local copies, waits for them, and re-layouts  27.5 us (7%)
  between operations  16 us (4%)
  other arithmetic  5.25 us (1%)
    psum x1, blocking collectives, per_device(): summed = lax.psum((numer, denom), 'blk')  125 us
    psum x1, blocking collectives, per_device(): totals, picked = lax.psum((totals, picked), ('blk', 'mp'))  64.9 us
    psum x1, waiting for transfers between devices, per_device(): lax.psum(jnp.dot(heads_out, out_weight, preferred_element_type=jnp.float3...  34.1 us
    all_gather x1, waiting for transfers between devices, per_device(): lax.all_gather(medusa_w, 'blk', axis=1, tiled=True)  32.7 us
    all_gather x1, waiting for transfers between devices, per_device(): full_fresh = lax.all_gather(fresh, 'mp', axis=2, tiled=True)  31.7 us
    dot_general x2, matrix products, attend(): jnp.einsum('qhrd,khd->hrqk', query_view, key_view, preferred_element_type...  11.3 us
    dot_general x2, matrix products, attend(): jnp.einsum('hrqk,khd->qhrd', weights.astype(jnp.bfloat16), value_view, pr...  9.63 us
    unnamed x19, local copies, waits for them, and re-layouts  7.84 us
  transfers between devices with their start and end apart: 4, of which 3 were waited for; matrix products, arithmetic and copies ran while one was open for 7% of the time, Pallas kernels for 0%

commit v1 on v0

--- a/solution.py
+++ b/solution.py
@@ -115,7 +115,10 @@
         .reshape(rows_dev, features)
         .astype(jnp.bfloat16)
     )
-    attn = lax.psum(jnp.dot(heads_out, out_weight, preferred_element_type=jnp.float32), "mp")
+    attn = jnp.sum(
+        lax.all_gather(jnp.dot(heads_out, out_weight, preferred_element_type=jnp.float32), "mp"),
+        axis=0,
+    )
     normed = attn * lax.rsqrt(jnp.mean(attn * attn, -1, keepdims=True) + 1e-06) * post_gain
     layer_out = (normed + resid.astype(jnp.float32)).astype(jnp.bfloat16)
     return (draft_logprob, layer_out)

time: 382 us -> 322 us (0.84)
  waiting for transfers between devices: 99.3 us -> 24.6 us
  blocking collectives: 190 us -> 205 us
    psum x1 -> x0, waiting for transfers between devices: 34.1 us -> none  [per_device(): lax.psum(jnp.dot(heads_out, out_weight, preferred_element_type=jnp.float3...]
    all_gather x1, waiting for transfers between devices: 31.7 us -> 0.01 us  [per_device(): full_fresh = lax.all_gather(fresh, 'mp', axis=2, tiled=True)]
    all_gather x0 -> x1, blocking collectives: none -> 14 us  [per_device(): lax.all_gather(jnp.dot(heads_out, out_weight, preferred_element_type=jnp....]
    all_gather x1, waiting for transfers between devices: 32.7 us -> 23.9 us  [per_device(): lax.all_gather(medusa_w, 'blk', axis=1, tiled=True)]
    psum x1, blocking collectives: 64.9 us -> 70.1 us  [per_device(): totals, picked = lax.psum((totals, picked), ('blk', 'mp'))]
  transfers between devices with their start and end apart: 4 -> 3, of which waited for: 3 -> 1; matrix products, arithmetic and copies ran while one was open for 7% -> 20% of each run, Pallas kernels for 0% -> 0%
where the time goes in v1:
time: 322 us
  blocking collectives  205 us (64%)
  matrix products  42.9 us (13%)
  local copies, waits for them, and re-layouts  28.4 us (9%)
  waiting for transfers between devices  24.6 us (8%)
  between operations  16 us (5%)
  other arithmetic  4.36 us (1%)
    psum x1, blocking collectives, per_device(): summed = lax.psum((numer, denom), 'blk')  121 us
    psum x1, blocking collectives, per_device(): totals, picked = lax.psum((totals, picked), ('blk', 'mp'))  70.1 us
    all_gather x1, waiting for transfers between devices, per_device(): lax.all_gather(medusa_w, 'blk', axis=1, tiled=True)  23.9 us
    all_gather x1, blocking collectives, per_device(): lax.all_gather(jnp.dot(heads_out, out_weight, preferred_element_type=jnp....  14 us
    dot_general x2, matrix products, attend(): jnp.einsum('qhrd,khd->hrqk', query_view, key_view, preferred_element_type...  12.1 us
    dot_general x2, matrix products, attend(): jnp.einsum('hrqk,khd->qhrd', weights.astype(jnp.bfloat16), value_view, pr...  9.64 us
    unnamed x19, local copies, waits for them, and re-layouts  8.62 us
    dot_general x1, matrix products, per_device(): jnp.einsum('rd,mdu->mru', hidden, lax.all_gather(medusa_w, 'blk', axis=1,...  7.92 us
  transfers between devices with their start and end apart: 3, of which 1 were waited for; matrix products, arithmetic and copies ran while one was open for 20% of the time, Pallas kernels for 0%

profile of v1, /device:TPU:1, one launch (start us, length us, event | category | flops | bytes accessed | tf_op | source)
XLA Modules:
  0.0 321.9 jit_solution(3027131254926797666)
XLA Ops:
  7.2 0.0 all-gather.5.cloned.1.call-start
  7.2 0.7 all-gather.5.cloned.1.call-update
  7.9 0.0 all-reduce.3.cloned.1.call-start
  7.9 4.4 %fusion.50 = (bf16[1,1,2048,512]{3,2,1,0:T(8,128)(2,1)}, bf16[1,1,2048,512]{3,2,1,0:T(8,128)(2,1)}) fusion(bf16[2,1,2048,512]{3,2,1,0:T(8,128)(2,1)} %param.20), kind=kLoop, calls=%fused_computation.70 | loop fusion | bytes 8388608 | tf_op jit(solution)/shard_map/slice | solution.py:88
  12.4 2.9 copy.79
  17.2 3.3 %reshape_reshape.3 = bf16[576,2,2,256]{3,2,1,0:T(2,128)(2,1)S(1)} reshape(bf16[12,48,1024]{2,1,0:T(8,128)(2,1)} %param.18) | data formatting | bytes 2359296 | tf_op jit(solution)/shard_map/reshape;reshape | solution.py:30
  20.6 4.0 %copy.80 = bf16[1,1,2048,512]{2,3,1,0:T(8,128)(2,1)} copy(bf16[1,1,2048,512]{3,2,1,0:T(8,128)(2,1)} %get-tuple-element.6) | data formatting | bytes 4194304
  24.6 0.4 broadcast_multiply_fusion
  25.0 9.9 %fusion = (f32[2,2,576]{2,1,0:T(2,128)S(1)}, f32[2,2048,576,2]{1,2,3,0:T(8,128)}) fusion(f32[576,2048]{1,0:T(8,128)S(1)} %broadcast_multiply_fusion, bf16[2048,2,256,1]{0,2,3,1:T(8,128)(2,1)S(1)} %bitcast.85, bf16[576,2,2,256]{3,2,1,0:T(2,128)(2,1)S(1)} %reshape_reshape.3), kind=kOutput, calls=%fused_computation.1 | convolution fusion | flops 2434791168 | bytes 26878976 | tf_op jit(solution)/shard_map/qhrd,khd->hrqk/dot_general | solution.py:33
  34.9 9.1 %fusion.6 = f32[576,2,2,256]{3,0,2,1:T(8,128)S(1)} fusion(bf16[2048,2,256,1]{0,2,3,1:T(8,128)(2,1)S(1)} %bitcast.87, f32[2,2048,576,2]{1,2,3,0:T(8,128)} %get-tuple-element.15, f32[576,2048]{1,0:T(8,128)S(1)} %broadcast_multiply_fusion), kind=kOutput, calls=%fused_computation.11 | convolution fusion | flops 2434793472 | bytes 28049408 | tf_op jit(solution)/shard_map/hrqk,khd->qhrd/dot_general | solution.py:38
  44.0 1.8 copy.56
  45.8 2.9 reshape.101
  48.7 0.0 all-reduce.3.cloned.1.call-update
  48.8 0.2 all-gather.7.cloned.1.call-start
  49.0 1.0 copy-done.2
  50.0 0.1 fusion.51
  50.1 0.6 convolution_minimum_fusion.5
  50.7 0.4 convolution_minimum_fusion.4
  51.1 0.4 convolution_minimum_fusion.3
  51.6 0.4 convolution_minimum_fusion.2
  52.0 1.0 dynamic-slice_convert_fusion
  53.0 0.4 convolution_minimum_fusion.1
  53.4 23.9 %all-gather.5.cloned.1.call-done = bf16[2,3584,896]{2,1,0:T(8,128)(2,1)} async-done(((bf16[2,112,896]{2,1,0:T(8,128)(2,1)}), bf16[2,3584,896]{2,1,0:T(8,128)(2,1)}) %all-gather.5.cloned.1.call-update) | async-done | bytes 12845072 | tf_op jit(solution)/shard_map/all_gather | solution.py:67
  77.3 7.9 %add_convert_fusion = bf16[2,144,896]{2,1,0:T(8,128)(2,1)} fusion(bf16[2,3584,896]{2,1,0:T(8,128)(2,1)} %all-gather.5.cloned.1.call-done, bf16[144,3584]{1,0:T(8,128)(2,1)} %param.14, f32[144,896]{1,0:T(8,128)S(1)} %dynamic-slice_convert_fusion), kind=kOutput, calls=%fused_computation.33 | convolution fusion | flops 1851236352 | bytes 14909440 | tf_op jit(solution)/shard_map/rd,mdu->mru/dot_general | solution.py:64
  85.2 0.4 convolution_minimum_fusion
  85.7 1.7 reshape.102
  87.4 0.1 reshape_squeeze.14
  87.5 0.1 copy.59
  87.7 2.2 fusion.52
  89.9 0.1 reshape.105
  90.0 121.3 %psum.31 = f32[576,4]{0,1:T(4,128)S(1)} all-reduce(f32[576,4]{0,1:T(4,128)S(1)} %reshape.104), channel_id=1, replica_groups=mesh['blk'=32,'mp'=4] {'blk'}, use_global_device_ids=true, to_apply=%region_6.7 | all-reduce | flops 2304 | bytes 18432 | tf_op jit(solution)/shard_map/psum | solution.py:99
  211.3 0.1 dynamic-slice_add_fusion
  211.4 0.1 copy.64
  211.5 0.1 div.48
  211.7 0.1 reshape_squeeze.15
  211.8 0.5 convolution_bitcast_fusion.1
  212.3 1.8 copy.62
  214.2 2.9 reshape.103
  217.1 0.0 all-reduce.3.cloned.1.call-done
  217.2 4.3 %convolution_bitcast_fusion = f32[1,18,3584]{2,1,0:T(8,128)S(1)} fusion(bf16[1024,3584]{1,0:T(8,128)(2,1)} %param.25, f32[18,1024]{1,0:T(8,128)S(1)} %bitcast.89, f32[576,1024]{1,0:T(8,128)} %reshape.103, s32[]{:T(128)S(6)} %select_n.25, f32[576,1024]{1,0:T(8,128)} %all-reduce.3.cloned.1.call-done), kind=kOutput, calls=%fused_computation.8 | convolution fusion | flops 132175872 | bytes 7868420 | tf_op jit(solution)/shard_map/dot_general | solution.py:119
  221.5 14.0 %all-gather.1 = f32[4,18,3584]{2,1,0:T(8,128)S(1)} all-gather(f32[1,18,3584]{2,1,0:T(8,128)S(1)} %convolution_bitcast_fusion), channel_id=2, replica_groups=mesh['blk'=32,'mp'=4] {'mp'}, dimensions={0}, use_global_device_ids=true | all-gather | bytes 1290240 | tf_op jit(solution)/shard_map/all_gather | solution.py:119
  235.5 0.1 reduce_sum.58
  235.6 0.1 multiply_reduce_fusion
  235.8 0.8 add_convert_fusion.1
  236.6 6.2 %exponential_reduce_fusion = (f32[2,144]{1,0:T(2,128)S(1)}, f32[2,144,1024]{2,1,0:T(8,128)S(1)}) fusion(bf16[2,144,3584]{2,1,0:T(8,128)(2,1)} %all-gather.7.cloned.1.call-done, bf16[1024,3584]{1,0:T(8,128)(2,1)} %param.16), kind=kOutput, calls=%fused_computation.25 | convolution fusion | flops 2114813696 | bytes 10585216 | tf_op jit(solution)/shard_map/mrd,vd->mrv/dot_general | solution.py:76
  242.8 1.8 select_reduce_fusion
  244.6 70.1 %all-reduce = (f32[2,144,10]{1,2,0:T(8,128)S(1)}, f32[2,144]{1,0:T(2,128)S(1)}) all-reduce(f32[2,144,10]{1,2,0:T(8,128)S(1)} %select_reduce_fusion, f32[2,144]{1,0:T(2,128)S(1)} %get-tuple-element.10), channel_id=1, replica_groups=mesh['blk'=32,'mp'=4] {'blk','mp'}, use_global_device_ids=true, to_apply=%region_1.2 | all-reduce | flops 3168 | bytes 25344 | tf_op jit(solution)/shard_map/psum | solution.py:84
  314.7 0.6 copy.65
  (28 shorter events, 0.2 us)
Async XLA Ops:
  7.2 70.1 %all-gather.5.cloned.1.call-start = ((), (), s32[]{:S(2)}) async-start(), calls=%async_computation | async-start | bytes 13246464 | tf_op jit(solution)/shard_map/all_gather | solution.py:67
  7.9 209.3 %all-reduce.3.cloned.1.call-start = ((), (), s32[]{:S(2)}) async-start(), calls=%async_computation.2 | async-start | bytes 4718592 | tf_op jit(solution)/shard_map/psum | solution.py:99
  25.0 9.9 %copy-start.1 = (bf16[1,1,2048,512]{2,3,1,0:T(8,128)(2,1)S(1)}, bf16[1,1,2048,512]{2,3,1,0:T(8,128)(2,1)}, u32[]{:S(2)}) copy-start(bf16[1,1,2048,512]{2,3,1,0:T(8,128)(2,1)} %copy.80) | copy-start | bytes 6291460
  48.7 1.3 copy-start.2
  48.7 1.4 copy-start.6
  48.8 187.8 %all-gather.7.cloned.1.call-start = ((), (), s32[]{:S(2)}) async-start(), calls=%async_computation.1 | async-start | bytes 2580480 | tf_op jit(solution)/shard_map/all_gather | solution.py:74
  53.4 32.2 %copy-start = (bf16[12,48,1024]{2,1,0:T(8,128)(2,1)S(1)}, bf16[12,48,1024]{2,1,0:T(8,128)(2,1)}, u32[]{:S(2)}) copy-start(bf16[12,48,1024]{2,1,0:T(8,128)(2,1)} %param.18) | copy-start | bytes 3538948
  214.1 3.0 copy-start.4
  221.5 14.3 %copy-start.3 = (bf16[18,3584]{1,0:T(8,128)(2,1)S(1)}, bf16[18,3584]{1,0:T(8,128)(2,1)}, u32[]{:S(2)}) copy-start(bf16[18,3584]{1,0:T(8,128)(2,1)} %param.27) | copy-start | bytes 387076
  221.5 14.3 %copy-start.5 = (f32[3584]{0:T(1024)S(1)}, f32[3584]{0:T(1024)}, u32[]{:S(2)}) copy-start(f32[3584]{0:T(1024)} %param.26) | copy-start | bytes 43012
Sparse Core Ops, SparseCore 0:
  10.4 66.8 all-gather.4
  80.6 106.3 all-reduce.2
  188.7 30.6 all-gather.6
